TPU v7x, 128 devices: a whole 4x4x4 slice. The times are simulated.
128 devices in a mesh: seq: 32 (over z, y, core), fsdp: 4 (over x).
Axes of the slice: x: 4, y: 4, z: 4, core: 2. Of those that a mesh axis runs over, the one named last changes fastest.
Arguments:
- self_query: bfloat16 [4, 8192, 2048], P('fsdp', 'seq'), may hold values from -8 to 8, as said below
- self_key: bfloat16 [4, 8192, 2048], P('fsdp', 'seq'), may hold values from -8 to 8, as said below
- self_value: bfloat16 [4, 8192, 2048], P('fsdp', 'seq'), may hold values from -6 to 6
- cross_query: bfloat16 [4, 8192, 2048], P('fsdp', 'seq'), may hold values from -6 to 6
- neighbours: bfloat16 [4, 128, 256, 768], P('fsdp', 'seq'), may hold values from -6 to 6
- neighbour_count: int32 [4, 128], P('fsdp', 'seq'), may hold values from 1 to 2
- kv_weight: bfloat16 [768, 4096], P('fsdp'), may hold values from -0.21875 to 0.21875
- out_grad: bfloat16 [4, 8192, 2048], P('fsdp', 'seq'), may hold values from -6 to 6
Outputs:
- block_out: bfloat16 [4, 8192, 2048], P('fsdp', 'seq')
- query_grad: bfloat16 [4, 8192, 2048], P('fsdp', 'seq')
- key_grad: bfloat16 [4, 8192, 2048], P('fsdp', 'seq')
- value_grad: bfloat16 [4, 8192, 2048], P('fsdp', 'seq')
- cross_grad: bfloat16 [4, 8192, 2048], P('fsdp', 'seq')
- weight_grad: float32 [768, 4096], P(('seq', 'fsdp'))
Inputs may be any that keep to these rules, and one draw needn't show every extreme that they name: `self_query`: entries of order one. `self_key`: entries of order one.
All inputs are finite; a program needn't handle non-finite values.
Results may differ from a plain program's by a relative error of at most 0.014.
Values may be sent and summed in bfloat16 or wider, within the bound.
A program may use at most 192 MiB of HBM per device.

v0:
```python
import jax
import jax.numpy as jnp
from jax import lax
from jax.sharding import PartitionSpec as P

HEADS = 16
HD = 128
GROUP = 64
RLEN = 128


neg_fill = -1e30


def from_behind(value, axis, steps):
    count = lax.axis_size(axis)
    first, last = (max(0, -steps), min(count, count - steps))
    return lax.ppermute(value, axis, [(source, source + steps) for source in range(first, last)])


def attend(queries, keys_in, values_in, grads, allowed, scaling):
    scores = (
        jnp.einsum("...qhd,...khd->...hqk", queries, keys_in, preferred_element_type=jnp.float32)
        * scaling
    )
    scores = jnp.where(allowed, scores, neg_fill)
    peaks = jnp.max(scores, axis=-1, keepdims=True)
    weights = jnp.exp(scores - peaks)
    probs = weights / jnp.sum(weights, axis=-1, keepdims=True)
    probs_low = probs.astype(jnp.bfloat16)
    output = jnp.einsum(
        "...hqk,...khd->...qhd", probs_low, values_in, preferred_element_type=jnp.float32
    )
    prob_grad = jnp.einsum(
        "...qhd,...khd->...hqk", grads, values_in, preferred_element_type=jnp.float32
    )
    row_delta = jnp.sum(probs * prob_grad, axis=-1, keepdims=True)
    score_grad = (probs * (prob_grad - row_delta) * scaling).astype(jnp.bfloat16)
    query_grad = jnp.einsum(
        "...hqk,...khd->...qhd", score_grad, keys_in, preferred_element_type=jnp.float32
    )
    key_grad = jnp.einsum(
        "...hqk,...qhd->...khd", score_grad, queries, preferred_element_type=jnp.float32
    )
    value_grad = jnp.einsum(
        "...hqk,...qhd->...khd", probs_low, grads, preferred_element_type=jnp.float32
    )
    return (output, query_grad, key_grad, value_grad)


def on_device(
    self_query, self_key, self_value, cross_query, neighbours, neighbour_count, kv_weight, out_grad
):
    tok_rows = self_query.shape[1]
    feature_width = self_query.shape[2]
    scaling = HD ** (-0.5)
    is_first = lax.axis_index("seq") == 0

    def head_view(array):
        return array.reshape(array.shape[:-1] + (HEADS, HD))

    prev_key, prev_value = from_behind((self_key, self_value), "seq", 1)
    all_keys = jnp.concatenate([prev_key[0], self_key[0]], 0)
    all_values = jnp.concatenate([prev_value[0], self_value[0]], 0)
    row_index = jnp.arange(tok_rows, dtype=jnp.int32)[:, None]
    col_index = jnp.arange(2 * tok_rows, dtype=jnp.int32)[None, :]
    self_allowed = (
        (col_index > row_index)
        & (col_index <= row_index + tok_rows)
        & ((col_index >= tok_rows) | jnp.logical_not(is_first))
    )
    self_out, self_qgrad, self_kterms, self_vterms = attend(
        head_view(self_query[0]),
        head_view(all_keys),
        head_view(all_values),
        head_view(out_grad[0]),
        self_allowed[None],
        scaling,
    )
    self_kterms = self_kterms.reshape(2 * tok_rows, feature_width)
    self_vterms = self_vterms.reshape(2 * tok_rows, feature_width)
    returned_key, returned_value = (
        from_behind(self_kterms[:tok_rows].astype(jnp.bfloat16), "seq", -1).astype(jnp.float32),
        from_behind(self_vterms[:tok_rows].astype(jnp.bfloat16), "seq", -1).astype(jnp.float32),
    )
    key_grad = (self_kterms[tok_rows:] + returned_key).astype(jnp.bfloat16)
    value_grad = (self_vterms[tok_rows:] + returned_value).astype(jnp.bfloat16)
    groups = tok_rows // GROUP
    encodings = neighbours[0]
    neigh_rows = encodings.shape[1]
    enc_width = encodings.shape[2]
    counts = neighbour_count[0].astype(jnp.bfloat16)
    rows_in = encodings.reshape(groups * neigh_rows, enc_width)
    columns = rows_in
    own_proj = (
        jnp.dot(
            columns,
            lax.all_gather(kv_weight, "fsdp", axis=0, tiled=True),
            preferred_element_type=jnp.float32,
        )
        .astype(jnp.bfloat16)
        .reshape(groups, neigh_rows, 2 * feature_width)
    )
    last_proj, last_count = from_behind((own_proj[groups - 1], counts[groups - 1 :]), "seq", 1)
    kv_proj = jnp.concatenate([last_proj[None], own_proj[: groups - 1]], 0)
    used_count = jnp.concatenate([last_count, counts[: groups - 1]], 0).astype(jnp.float32)
    neighbour_of = (jnp.arange(neigh_rows, dtype=jnp.int32) // RLEN).astype(jnp.float32)
    cross_allowed = (neighbour_of[None, :] < used_count[:, None])[:, None, None, :]
    group_keys = kv_proj[..., :feature_width].reshape(groups, neigh_rows, HEADS, HD)
    group_values = kv_proj[..., feature_width:].reshape(groups, neigh_rows, HEADS, HD)
    group_view = (groups, GROUP, HEADS, HD)
    cross_out, cross_qgrad, cross_kgrad, cross_vgrad = attend(
        cross_query[0].reshape(group_view),
        group_keys,
        group_values,
        out_grad[0].reshape(group_view),
        cross_allowed,
        scaling,
    )
    group_live = (jnp.arange(groups, dtype=jnp.int32) > 0) | jnp.logical_not(is_first)
    live_rows = group_live[:, None, None, None]
    cross_out = jnp.where(live_rows, cross_out, 0.0)
    cross_qgrad = jnp.where(live_rows, cross_qgrad, 0.0)
    kv_grad = jnp.concatenate(
        [
            cross_kgrad.reshape(groups, neigh_rows, feature_width),
            cross_vgrad.reshape(groups, neigh_rows, feature_width),
        ],
        -1,
    )
    kv_grad = jnp.where(group_live[:, None, None], kv_grad, 0.0).astype(jnp.bfloat16)
    returned_kv = from_behind(kv_grad[0], "seq", -1)
    grad_rows = encodings.reshape(groups * neigh_rows, enc_width)
    grad_kv = jnp.concatenate([kv_grad[1:], returned_kv[None]], 0).reshape(
        groups * neigh_rows, 2 * feature_width
    )
    columns = grad_rows
    weight_grad = lax.psum_scatter(
        jnp.einsum("re,rc->ec", columns, grad_kv, preferred_element_type=jnp.float32),
        ("seq", "fsdp"),
        scatter_dimension=0,
        tiled=True,
    )
    block_out = (
        self_out.reshape(tok_rows, feature_width) + cross_out.reshape(tok_rows, feature_width)
    ).astype(jnp.bfloat16)
    query_grad = self_qgrad.reshape(tok_rows, feature_width).astype(jnp.bfloat16)
    cross_grad = cross_qgrad.reshape(tok_rows, feature_width).astype(jnp.bfloat16)
    return (
        block_out[None],
        query_grad[None],
        key_grad[None],
        value_grad[None],
        cross_grad[None],
        weight_grad,
    )


def solution(mesh):
    in_specs = (
        P("fsdp", "seq", None),
        P("fsdp", "seq", None),
        P("fsdp", "seq", None),
        P("fsdp", "seq", None),
        P("fsdp", "seq", None, None),
        P("fsdp", "seq"),
        P("fsdp", None),
        P("fsdp", "seq", None),
    )
    out_specs = (
        P("fsdp", "seq", None),
        P("fsdp", "seq", None),
        P("fsdp", "seq", None),
        P("fsdp", "seq", None),
        P("fsdp", "seq", None),
        P(("seq", "fsdp"), None),
    )
    return jax.shard_map(
        on_device, mesh=mesh, in_specs=in_specs, out_specs=out_specs, check_vma=False
    )
```

profile of v0, /device:TPU:1, one launch (start us, length us, event | category | flops | bytes accessed | tf_op | source)
XLA Modules:
  0.0 452.9 jit_solution(12350276214869502606)
XLA Ops:
  8.0 70.4 %all-gather.2.cloned.1.call-done = bf16[768,4096]{1,0:T(8,128)(2,1)} async-done(((bf16[192,4096]{1,0:T(8,128)(2,1)}), bf16[768,4096]{1,0:T(8,128)(2,1)}) %all-gather.2.cloned.1.call-update) | async-done | bytes 6291472 | tf_op jit(solution)/shard_map/all_gather | solution.py:98
  78.3 9.9 %convolution_convert_fusion = bf16[1024,4096]{1,0:T(8,128)(2,1)S(1)} fusion(bf16[1024,768]{1,0:T(8,128)(2,1)S(1)} %bitcast.154, bf16[768,4096]{1,0:T(8,128)(2,1)} %all-gather.2.cloned.1.call-done), kind=kOutput, calls=%fused_computation.17 | convolution fusion | flops 6446645248 | bytes 16252928 | tf_op jit(solution)/shard_map/dot_general | solution.py:96
  100.7 4.0 collective-permute-start.1
  108.6 11.6 %collective-permute-done.3 = bf16[1]{0:T(256)(128)(2,1)} collective-permute-done((bf16[1]{0:T(256)(128)(2,1)}, bf16[1]{0:T(256)(128)(2,1)}, u32[]{:S(2)}, u32[]{:S(2)}) %collective-permute-start.3) | collective-permute-done | bytes 34 | tf_op jit(solution)/shard_map/ppermute | solution.py:18
  120.9 6.3 %slice.74 = bf16[768,4096]{1,0:T(8,128)(2,1)} slice(bf16[1024,4096]{1,0:T(8,128)(2,1)} %copy-done.6), slice={[0:768], [0:4096]} | slice | bytes 12582912 | tf_op jit(solution)/shard_map/slice | solution.py:105
  127.2 8.6 %copy.83 = bf16[3,256,4096]{1,2,0:T(8,128)(2,1)} copy(bf16[3,256,4096]{2,1,0:T(8,128)(2,1)} %bitcast.158) | data formatting | bytes 12582912 | tf_op jit(solution)/shard_map/slice | solution.py:105
  135.8 4.1 copy.82
  139.9 4.0 pad_maximum_fusion.1
  156.0 30.6 %fusion.31 = bf16[4,16,256,128]{2,3,1,0:T(8,128)(2,1)} fusion(f32[4,16,256,64]{2,3,1,0:T(8,128)} %fusion.43, bf16[4,64,16,128]{3,2,1,0:T(8,128)(2,1)S(1)} %bitcast.167, f32[4,16,64,256]{3,2,1,0:T(8,128)} %copy-done.18, f32[4,16,64]{2,1,0:T(8,128)S(1)} %get-tuple-element.28), kind=kOutput, calls=%fused_computation.58 | convolution fusion | flops 275779840 | bytes 13647872 | tf_op jit(solution)/shard_map/...hqk,...qhd->...khd/dot_general | solution.py:42
  186.6 6.3 %copy.108 = bf16[4,256,2048]{2,1,0:T(8,128)(2,1)} copy(bf16[4,256,2048]{1,2,0:T(8,128)(2,1)} %bitcast.170) | data formatting | bytes 8388608 | tf_op jit(solution)/shard_map/reshape | solution.py:127
  192.9 6.3 %copy.107 = bf16[4,256,2048]{2,1,0:T(8,128)(2,1)} copy(bf16[4,256,2048]{1,2,0:T(8,128)(2,1)} %bitcast.171) | data formatting | bytes 8388608 | tf_op jit(solution)/shard_map/reshape | solution.py:126
  199.1 5.0 %fusion.4 = bf16[4,256,4096]{2,1,0:T(8,128)(2,1)S(1)} fusion(bf16[4,256,2048]{2,1,0:T(8,128)(2,1)} %copy.108, bf16[4,256,2048]{2,1,0:T(8,128)(2,1)} %copy.107, pred[4]{0:T(512)(128)(4,1)S(1)} %compare_or_fusion), kind=kLoop, calls=%fused_computation.5 | loop fusion | flops 20971520 | bytes 16777220 | tf_op jit(solution)/shard_map/convert_element_type | solution.py:131
  210.9 4.7 %collective-permute-start = (bf16[1,256,2048]{2,1,0:T(8,128)(2,1)}, bf16[1,256,2048]{2,1,0:T(8,128)(2,1)}, u32[]{:S(2)}, u32[]{:S(2)}) collective-permute-start(bf16[1,256,2048]{2,1,0:T(8,128)(2,1)} %param.10), channel_id=1, source_target_pairs={{0,4},{4,8},{8,12},{12,16},{16,20},{20,24},{24,28},{28,32},{32,36}... | collective-permute-start | bytes 3145736 | tf_op jit(solution)/shard_map/ppermute | solution.py:18
  229.1 5.6 %fusion.68 = (f32[16,256]{1,0:T(8,128)S(1)}, f32[16,256,512]{1,2,0:T(8,128)}) fusion(f32[16,512,256]{2,1,0:T(8,128)S(1)} %fusion.34, pred[256,512]{0,1:T(8,128)(4,1)S(1)} %copy-done.16), kind=kOutput, calls=%fused_computation.108 | output fusion | flops 12583423 | bytes 16924672 | tf_op jit(solution)/shard_map/sub | solution.py:28
  237.7 7.4 %pad_maximum_fusion = bf16[4,256,4096]{2,1,0:T(8,128)(2,1)} fusion(bf16[1,256,4096]{2,1,0:T(8,128)(2,1)} %bitcast.34, bf16[3,256,4096]{2,1,0:T(8,128)(2,1)} %slice.81), kind=kLoop, calls=%fused_computation.8 | loop fusion | flops 4194304 | bytes 16777216 | tf_op jit(solution)/shard_map/concatenate | solution.py:134
  245.1 12.9 %convolution_bitcast_fusion = f32[768,4096]{0,1:T(8,128)} fusion(bf16[1024,4096]{1,0:T(8,128)(2,1)} %bitcast.163, bf16[1024,768]{1,0:T(8,128)(2,1)S(1)} %bitcast.155), kind=kOutput, calls=%fused_computation.16 | convolution fusion | flops 6442450944 | bytes 22544384 | tf_op jit(solution)/shard_map/re,rc->ec/dot_general | solution.py:139
  259.2 4.9 %convolution_bitcast_fusion.1 = f32[512,16,128]{0,2,1:T(8,128)S(1)} fusion(bf16[256,16,128]{0,2,1:T(8,128)(2,1)S(1)} %bitcast.178, f32[16,256,512]{1,2,0:T(8,128)} %get-tuple-element.27, f32[16,256]{1,0:T(8,128)S(1)} %get-tuple-element.26), kind=kOutput, calls=%fused_computation.39 | convolution fusion | flops 541065216 | bytes 13647872 | tf_op jit(solution)/shard_map/...hqk,...qhd->...khd/dot_general | solution.py:45
  270.1 6.5 %fusion.35 = f32[16,512,256]{2,1,0:T(8,128)} fusion(bf16[256,16,128]{0,2,1:T(8,128)(2,1)} %bitcast.177, bf16[256,16,128]{0,2,1:T(8,128)(2,1)} %bitcast.175, bf16[256,16,128]{0,2,1:T(8,128)(2,1)} %bitcast.181), kind=kOutput, calls=%fused_computation.62 | convolution fusion | flops 541065216 | bytes 11534336 | tf_op jit(solution)/shard_map/...qhd,...khd->...hqk/dot_general | solution.py:34
  276.6 15.0 %fusion.23 = f32[512,16,128]{0,2,1:T(8,128)} fusion(bf16[256,16,128]{0,2,1:T(8,128)(2,1)S(1)} %bitcast.180, f32[16,512,256]{2,1,0:T(8,128)} %fusion.35, f32[16,256,512]{1,2,0:T(8,128)} %get-tuple-element.27, f32[16,256]{1,0:T(8,128)S(1)} %get-tuple-element.26), kind=kOutput, calls=%fused_computation.38 | convolution fusion | flops 551555584 | bytes 22036480 | tf_op jit(solution)/shard_map/...hqk,...qhd->...khd/dot_general | solution.py:42
  298.9 6.5 %fusion.27 = f32[16,128,256]{2,1,0:T(8,128)} fusion(bf16[256,16,128]{0,2,1:T(8,128)(2,1)} %bitcast.176, bf16[256,16,128]{0,2,1:T(8,128)(2,1)} %bitcast.182, f32[16,256,512]{1,2,0:T(8,128)} %get-tuple-element.27, f32[16,256]{1,0:T(8,128)S(1)} %get-tuple-element.26), kind=kOutput, calls=%fused_computation.54 | convolution fusion | flops 545259520 | bytes 12599296 | tf_op jit(solution)/shard_map/...hqk,...khd->...qhd/dot_general | solution.py:31
  308.6 14.6 %fusion.33 = bf16[16,128,256]{2,1,0:T(8,128)(2,1)} fusion(f32[16,512,256]{2,1,0:T(8,128)} %fusion.35, bf16[256,16,128]{2,0,1:T(8,128)(2,1)S(1)} %copy.79, bf16[256,16,128]{2,0,1:T(8,128)(2,1)S(1)} %copy-done.9, f32[16,256,512]{1,2,0:T(8,128)} %get-tuple-element.27, f32[16,256]{1,0:T(8,128)S(1)} %get-tuple-element.26), kind=kOutput, calls=%fused_computation.60 | convolution fusion | flops 556274176 | bytes 19939328 | tf_op jit(solution)/shard_map/...hqk,...khd->...qhd/dot_general | solution.py:39
  348.2 29.5 %fusion.36 = bf16[4,64,16,128]{3,1,2,0:T(8,128)(2,1)S(1)} fusion(bf16[4,256,16,128]{1,3,2,0:T(8,128)(2,1)} %bitcast.160, f32[4,16,256,64]{2,3,1,0:T(8,128)} %fusion.43, pred[4]{0:T(512)(128)(4,1)S(1)} %compare_or_fusion, f32[4,16,64,256]{3,2,1,0:T(8,128)} %copy-done.18, f32[4,16,64]{2,1,0:T(8,128)S(1)} %copy-done.21), kind=kOutput, calls=%fused_computation.63 | convolution fusion | flops 276828416 | bytes 13647876 | tf_op jit(solution)/shard_map/...hqk,...khd->...qhd/dot_general | solution.py:39
  383.3 55.6 %all-reduce.3.cloned.1.call-done = f32[768,4096]{0,1:T(8,128)} async-done(((f32[768,4096]{0,1:T(8,128)}), f32[768,4096]{0,1:T(8,128)}) %all-reduce.3.cloned.1.call-update) | async-done | bytes 12582928
  438.8 4.1 constant_dynamic-slice_fusion
  (110 shorter events, 104.3 us)
Async XLA Ops:
  7.2 71.2 %copy-start = (bf16[1,4,256,768]{3,2,1,0:T(8,128)(2,1)S(1)}, bf16[1,4,256,768]{3,2,1,0:T(8,128)(2,1)}, u32[]{:S(2)}) copy-start(bf16[1,4,256,768]{3,2,1,0:T(8,128)(2,1)} %param.12) | copy-start | bytes 4718596
  7.2 71.1 %all-gather.2.cloned.1.call-start = ((), (), s32[]{:S(2)}) async-start(), calls=%async_computation | async-start | bytes 7864320 | tf_op jit(solution)/shard_map/all_gather | solution.py:98
  7.9 430.9 %all-reduce.3.cloned.1.call-start = ((), (), s32[]{:S(2)}) async-start(), calls=%async_computation.1 | async-start | bytes 25165824
  91.5 5.4 %copy-start.17 = (s32[1,4]{1,0:T(1,128)S(1)}, s32[1,4]{1,0:T(1,128)}, u32[]{:S(2)}) copy-start(s32[1,4]{1,0:T(1,128)} %param.13) | copy-start | bytes 52
  91.5 7.9 %copy-start.15 = (bf16[1,256,2048]{2,1,0:T(8,128)(2,1)S(1)}, bf16[1,256,2048]{2,1,0:T(8,128)(2,1)}, u32[]{:S(2)}) copy-start(bf16[1,256,2048]{2,1,0:T(8,128)(2,1)} %param.9) | copy-start | bytes 3145732
  93.0 42.8 %collective-permute-start.2 = (bf16[256,4096]{1,0:T(8,128)(2,1)}, bf16[256,4096]{1,0:T(8,128)(2,1)}, u32[]{:S(2)}, u32[]{:S(2)}) collective-permute-start(bf16[256,4096]{1,0:T(8,128)(2,1)} %slice.73), channel_id=1, source_target_pairs={{0,4},{4,8},{8,12},{12,16},{16,20},{20,24},{24,28},{28,32},{32,36}... | collective-permute-start | bytes 6291464 | tf_op jit(solution)/shard_map/ppermute | solution.py:18
  97.4 22.7 %collective-permute-start.3 = (bf16[1]{0:T(256)(128)(2,1)}, bf16[1]{0:T(256)(128)(2,1)}, u32[]{:S(2)}, u32[]{:S(2)}) collective-permute-start(bf16[1]{0:T(256)(128)(2,1)} %bitcast.11), channel_id=1, source_target_pairs={{0,4},{4,8},{8,12},{12,16},{16,20},{20,24},{24,28},{28,32},{32,36}... | collective-permute-start | bytes 14 | tf_op jit(solution)/shard_map/ppermute | solution.py:18
  100.7 123.2 %collective-permute-start.1 = (bf16[1,256,2048]{1,2,0:T(8,128)(2,1)}, bf16[1,256,2048]{1,2,0:T(8,128)(2,1)}, u32[]{:S(2)}, u32[]{:S(2)}) collective-permute-start(bf16[1,256,2048]{1,2,0:T(8,128)(2,1)} %copy.76), channel_id=1, source_target_pairs={{0,4},{4,8},{8,12},{12,16},{16,20},{20,24},{24,28},{28,32},{32,36}... | collective-permute-start | bytes 3145736 | tf_op jit(solution)/shard_map/ppermute | solution.py:18
  143.9 4.5 copy-start.3
  150.9 5.1 %copy-start.20 = (f32[4,16,64]{2,1,0:T(8,128)}, f32[4,16,64]{2,1,0:T(8,128)S(1)}, u32[]{:S(2)}) copy-start(f32[4,16,64]{2,1,0:T(8,128)S(1)} %get-tuple-element.28) | copy-start | bytes 49156
  207.4 10.5 %copy-start.8 = (bf16[1,256,2048]{2,1,0:T(8,128)(2,1)S(1)}, bf16[1,256,2048]{2,1,0:T(8,128)(2,1)}, u32[]{:S(2)}) copy-start(bf16[1,256,2048]{2,1,0:T(8,128)(2,1)} %param.15) | copy-start | bytes 3145732
  209.0 28.8 %collective-permute-start.6 = (bf16[256,4096]{1,0:T(8,128)(2,1)}, bf16[256,4096]{1,0:T(8,128)(2,1)}, u32[]{:S(2)}, u32[]{:S(2)}) collective-permute-start(bf16[256,4096]{1,0:T(8,128)(2,1)} %slice_bitcast_fusion), channel_id=1, source_target_pairs={{4,0},{8,4},{12,8},{16,12},{20,16},{24,20},{28,24},{32,28},{36,32}... | collective-permute-start | bytes 6291464 | tf_op jit(solution)/shard_map/ppermute | solution.py:18
  210.9 56.7 %collective-permute-start = (bf16[1,256,2048]{2,1,0:T(8,128)(2,1)}, bf16[1,256,2048]{2,1,0:T(8,128)(2,1)}, u32[]{:S(2)}, u32[]{:S(2)}) collective-permute-start(bf16[1,256,2048]{2,1,0:T(8,128)(2,1)} %param.10), channel_id=1, source_target_pairs={{0,4},{4,8},{8,12},{12,16},{16,20},{20,24},{24,28},{28,32},{32,36}... | collective-permute-start | bytes 3145736 | tf_op jit(solution)/shard_map/ppermute | solution.py:18
  226.1 8.5 %slice-start = ((s8[8388608]{0:T(1024)(128)(4,1)}), s8[4194304]{0:T(1024)(128)(4,1)S(1)}, s32[]{:S(2)}) async-start(s8[8388608]{0:T(1024)(128)(4,1)} %bitcast.156), calls=%async_computation.2 | async-start | bytes 8388608
  229.0 5.6 %slice-start.1 = ((s8[8388608]{0:T(1024)(128)(4,1)}), s8[4194304]{0:T(1024)(128)(4,1)S(1)}, s32[]{:S(2)}) async-start(s8[8388608]{0:T(1024)(128)(4,1)} %bitcast.156), calls=%async_computation.3 | async-start | bytes 8388608
  270.1 6.5 %copy-start.11 = (bf16[1,256,2048]{1,2,0:T(8,128)(2,1)S(1)}, bf16[1,256,2048]{1,2,0:T(8,128)(2,1)}, u32[]{:S(2)}) copy-start(bf16[1,256,2048]{1,2,0:T(8,128)(2,1)} %copy.123) | copy-start | bytes 3145732
  294.8 10.6 %copy-start.13 = (f32[512,16,128]{0,2,1:T(8,128)S(1)}, f32[512,16,128]{0,2,1:T(8,128)}, u32[]{:S(2)}) copy-start(f32[512,16,128]{0,2,1:T(8,128)} %copy-done.12) | copy-start | bytes 12582916
  294.8 39.5 %collective-permute-start.4 = (bf16[256,2048]{1,0:T(8,128)(2,1)}, bf16[256,2048]{1,0:T(8,128)(2,1)}, u32[]{:S(2)}, u32[]{:S(2)}) collective-permute-start(bf16[256,2048]{1,0:T(8,128)(2,1)} %copy.95), channel_id=1, source_target_pairs={{4,0},{8,4},{12,8},{16,12},{20,16},{24,20},{28,24},{32,28},{36,32}... | collective-permute-start | bytes 3145736 | tf_op jit(solution)/shard_map/ppermute | solution.py:18
  296.9 40.6 %collective-permute-start.5 = (bf16[256,2048]{1,0:T(8,128)(2,1)}, bf16[256,2048]{1,0:T(8,128)(2,1)}, u32[]{:S(2)}, u32[]{:S(2)}) collective-permute-start(bf16[256,2048]{1,0:T(8,128)(2,1)} %copy.99), channel_id=1, source_target_pairs={{4,0},{8,4},{12,8},{16,12},{20,16},{24,20},{28,24},{32,28},{36,32}... | collective-permute-start | bytes 3145736 | tf_op jit(solution)/shard_map/ppermute | solution.py:18
  298.9 8.1 %copy-start.14 = (f32[512,16,128]{0,2,1:T(8,128)S(1)}, f32[512,16,128]{0,2,1:T(8,128)}, u32[]{:S(2)}) copy-start(f32[512,16,128]{0,2,1:T(8,128)} %fusion.23) | copy-start | bytes 12582916
  331.3 9.8 %copy-start.21 = (f32[4,16,64]{2,1,0:T(8,128)S(1)}, f32[4,16,64]{2,1,0:T(8,128)}, u32[]{:S(2)}) copy-start(f32[4,16,64]{2,1,0:T(8,128)} %copy-done.20) | copy-start | bytes 49156
  334.2 6.9 %copy-start.5 = (bf16[4,256,2048]{1,2,0:T(8,128)(2,1)S(1)}, bf16[4,256,2048]{1,2,0:T(8,128)(2,1)}, u32[]{:S(2)}) copy-start(bf16[4,256,2048]{1,2,0:T(8,128)(2,1)} %copy-done.4) | copy-start | bytes 12582916
  334.2 6.9 %copy-start.19 = (f32[4,16,64,256]{3,2,1,0:T(8,128)S(1)}, f32[4,16,64,256]{3,2,1,0:T(8,128)}, u32[]{:S(2)}) copy-start(f32[4,16,64,256]{3,2,1,0:T(8,128)} %copy-done.18) | copy-start | bytes 12582916
  379.7 66.2 %copy-start.1 = (bf16[1,4,256,768]{3,2,1,0:T(8,128)(2,1)S(1)}, bf16[1,4,256,768]{3,2,1,0:T(8,128)(2,1)}, u32[]{:S(2)}) copy-start(bf16[1,4,256,768]{3,2,1,0:T(8,128)(2,1)} %param.12) | copy-start | bytes 4718596
  (9 other events, 25.0 us)
Sparse Core Ops, SparseCore 0:
  9.7 68.6 all-gather.1
  258.1 180.6 all-reduce.2
where the time goes:
time: 457 us; the launch traced here: 453 us
  matrix products  142 us (31%)
  waiting for transfers between devices  138 us (30%)
  local copies, waits for them, and re-layouts  102 us (22%)
  other arithmetic  35.8 us (8%)
  starting transfers between devices  20.4 us (4%)
  between operations  14.6 us (3%)
    all_gather x1, waiting for transfers between devices, on_device(): lax.all_gather(kv_weight, 'fsdp', axis=0, tiled=True)  70.4 us
    unnamed x3, waiting for transfers between devices  56.3 us
    dot_general x2, matrix products, attend(): jnp.einsum('...hqk,...qhd->...khd', score_grad, queries, preferred_elemen...  45.6 us
    dot_general x2, matrix products, attend(): jnp.einsum('...hqk,...khd->...qhd', score_grad, keys_in, preferred_elemen...  44.1 us
    unnamed x55, local copies, waits for them, and re-layouts  29.6 us
    ppermute x7, starting transfers between devices, from_behind(): lax.ppermute(value, axis, [(source, source + steps) for source in range(f...  20.3 us
    slice x2, local copies, waits for them, and re-layouts, on_device(): kv_proj = jnp.concatenate([last_proj[None], own_proj[:groups - 1]], 0)  14.9 us
    dot_general x1, matrix products, on_device(): jnp.einsum('re,rc->ec', columns, grad_kv, preferred_element_type=jnp.floa...  12.9 us
  transfers between devices with their start and end apart: 9, of which 3 were waited for; matrix products, arithmetic and copies ran while one was open for 55% of the time, Pallas kernels for 0%

commit v1 on v0

v1 whole, which is shorter than its diff:
```python
import jax
import jax.numpy as jnp
from jax import lax
from jax.experimental import pallas as pl
from jax.experimental.pallas import tpu as pltpu
from jax.sharding import PartitionSpec as P

HEADS = 16
HD = 128
GROUP = 64
RLEN = 128
ROWS = 256
WIDTH = HEADS * HD
ENC = 768
SHARD = 192
SEQ = 32
FSDP = 4
NEG = -1e30
SCALE = HD ** -0.5
EXP_SCALE = SCALE * 1.4426950408889634
F32 = jnp.float32
BF16 = jnp.bfloat16
MESH = pl.DeviceIdType.MESH
PIECES = 4
PIECE = WIDTH // PIECES


def dot(a, b, contract):
    return lax.dot_general(a, b, (contract, ((), ())), preferred_element_type=F32)


def head_cols(h):
    return pl.ds(pl.multiple_of(h * HD, HD), HD)


def kernel(
    q_hbm, k_hbm, v_hbm, cq_hbm, nb_hbm, cnt_hbm, w_hbm, og_hbm,
    bo_hbm, qg_hbm, kg_hbm, vg_hbm, cg_hbm, wg_hbm,
    qb, ogb, cqb, kbuf, vbuf, so, qgb, kgb, vgb, cgb, bob,
    dps, dpr, dko, dvo, W, N4, NT, cown, cprev, mb, kvb, kvg,
    pbuf, r0, sb1, r1, sb2, r2, f3, sb3, own3, r3, wout,
    lsem, hs, hr, ns, nr, wos, wor, wfs, wfr, wps, wpr, dss, drr, osem,
    s0s, s0r, s1s, s1r, s2s, s2r, s3s, s3r,
):
    s = lax.axis_index("seq")
    x = lax.axis_index("fsdp")
    c = lax.rem(s, 2)
    y = lax.rem(lax.div(s, 2), 4)
    z = lax.div(s, 8)
    nxt = lax.rem(s + 1, SEQ)
    prv = lax.rem(s + SEQ - 1, SEQ)
    other = s + 1 - 2 * c
    xp = lax.rem(x + 1, FSDP)
    xm = lax.rem(x + FSDP - 1, FSDP)
    pri = z * (1 - c) + y * c
    sec = y * (1 - c) + z * c
    step1 = 8 * (1 - c) + 2 * c
    step2 = 2 * (1 - c) + 8 * c

    def remote(src, dst, send, recv, dev):
        return pltpu.make_async_remote_copy(
            src_ref=src, dst_ref=dst, send_sem=send, recv_sem=recv, device_id=dev, device_id_type=MESH
        )

    def shard_rows(at):
        return pl.ds(pl.multiple_of(at * SHARD, 16), SHARD)

    locals_in = [
        pltpu.make_async_copy(q_hbm, qb, lsem.at[0]),
        pltpu.make_async_copy(og_hbm, ogb, lsem.at[1]),
        pltpu.make_async_copy(k_hbm, kbuf.at[pl.ds(ROWS, ROWS)], lsem.at[2]),
        pltpu.make_async_copy(v_hbm, vbuf.at[pl.ds(ROWS, ROWS)], lsem.at[3]),
        pltpu.make_async_copy(cnt_hbm, cown, lsem.at[4]),
        pltpu.make_async_copy(nb_hbm.at[pl.ds(0, 768)], N4.at[pl.ds(256, 768)], lsem.at[5]),
        pltpu.make_async_copy(cq_hbm, cqb, lsem.at[6]),
        pltpu.make_async_copy(w_hbm, W.at[shard_rows(x)], lsem.at[7]),
    ]
    for copy in locals_in:
        copy.start()

    barrier = pltpu.get_barrier_semaphore()
    peers = [(nxt, x), (prv, x), (other, x)]
    for d in range(1, 4):
        peers.append((s + (lax.rem(pri + d, 4) - pri) * step1, x))
        peers.append((s + (lax.rem(sec + d, 4) - sec) * step2, x))
        peers.append((s, lax.rem(x + d, FSDP)))
        peers.append((other, lax.rem(x + d, FSDP)))
    for dev in peers:
        pl.semaphore_signal(barrier, inc=1, device_id=dev, device_id_type=MESH)

    first = s == 0
    for r in range(2):
        row = lax.broadcasted_iota(jnp.int32, (128, 384), 0)
        col = lax.broadcasted_iota(jnp.int32, (128, 384), 1)
        least = jnp.where(first, 256 - 128 * r, 0)
        ok = (col > row) & (col <= row + 256) & (col >= least)
        mb[r] = jnp.where(ok, 0.0, NEG)
    f3[...] = jnp.zeros_like(f3)

    pl.semaphore_wait(barrier, len(peers))

    def piece_cols(half, j):
        return pl.ds(pl.multiple_of(half * WIDTH + j * PIECE, PIECE), PIECE)

    def own_piece(j, side):
        dst = W.at[shard_rows(x), piece_cols(c, j)]
        return remote(w_hbm.at[:, piece_cols(c, j)], dst, wos.at[side, j], wor.at[side, j], (s, (xp, xm)[side]))

    def passed_on(j):
        side = 0 if j < PIECES // 2 else 1
        at = W.at[shard_rows((xm, xp)[side]), piece_cols(c, j)]
        return remote(at, at, wfs.at[j], wfr.at[j], (s, (xp, xm)[side]))

    def to_other(j, d):
        at = W.at[shard_rows(lax.rem(x + d, FSDP)), piece_cols(c, j)]
        return remote(at, at, wps.at[d - 1, j], wpr.at[d - 1, j], (other, x))

    def halo(h):
        cols = head_cols(h)
        return [
            remote(k_hbm.at[:, cols], kbuf.at[pl.ds(0, ROWS), cols], hs.at[0], hr.at[0, h], (nxt, x)),
            remote(v_hbm.at[:, cols], vbuf.at[pl.ds(0, ROWS), cols], hs.at[1], hr.at[1, h], (nxt, x)),
        ]

    halo_nb = remote(nb_hbm.at[pl.ds(768, 256)], N4.at[pl.ds(0, 256)], ns.at[0], nr.at[0], (nxt, x))
    halo_cnt = remote(cnt_hbm, cprev, ns.at[1], nr.at[1], (nxt, x))

    for j in range(2):
        for side in range(2):
            own_piece(j, side).start()

    @pl.loop(0, HEADS)
    def _(h):
        for copy in halo(h):
            copy.start()

    halo_nb.start()
    halo_cnt.start()

    for copy in locals_in[:4]:
        copy.wait()

    def grad_return(h):
        return remote(dps.at[h], dpr.at[h], dss.at[0], drr.at[h], (prv, x))

    def column_out(buf, hbm, at, h):
        return pltpu.make_async_copy(buf.at[:, head_cols(h)], hbm.at[:, head_cols(h)], osem.at[at])

    @pl.loop(0, HEADS)
    def _(h):
        cols = head_cols(h)
        for copy in halo(h):
            copy.wait_recv()
        dk = []
        dv = []
        for r in range(2):
            rows = pl.ds(128 * r, 128)
            span = pl.ds(128 * r, 384)
            q = qb[rows, cols]
            og = ogb[rows, cols]
            kk = kbuf[span, cols]
            vv = vbuf[span, cols]
            raw = dot(q, kk, ((1,), (1,))) + mb[r]
            e = jnp.exp2((raw - jnp.max(raw, axis=1, keepdims=True)) * EXP_SCALE)
            p = e * (1.0 / jnp.sum(e, axis=1, keepdims=True))
            low = p.astype(BF16)
            so[rows, cols] = dot(low, vv, ((1,), (0,)))
            gp = dot(og, vv, ((1,), (1,)))
            sg = (p * (gp - jnp.sum(p * gp, axis=1, keepdims=True))).astype(BF16)
            qgb[rows, cols] = (dot(sg, kk, ((1,), (0,))) * SCALE).astype(BF16)
            dk.append(dot(sg, q, ((0,), (0,))) * SCALE)
            dv.append(dot(low, og, ((0,), (0,))))
        column_out(qgb, qg_hbm, 1, h).start()
        for at, (terms, own) in enumerate(((dk, dko), (dv, dvo))):
            dps[h, at, 0:128] = terms[0][0:128].astype(BF16)
            dps[h, at, 128:256] = (terms[0][128:256] + terms[1][0:128]).astype(BF16)
            own[h, 0:128] = terms[0][256:384] + terms[1][128:256]
            own[h, 128:256] = terms[1][256:384]
        grad_return(h).start()

        @pl.when(h == 4)
        def _():
            own_piece(0, 0).wait_recv()
            own_piece(0, 1).wait_recv()
            passed_on(0).start()
            own_piece(2, 0).start()
            own_piece(2, 1).start()
            to_other(0, 3).start()
            to_other(0, 1).start()

        @pl.when(h == 7)
        def _():
            own_piece(1, 0).wait_recv()
            own_piece(1, 1).wait_recv()
            passed_on(1).start()
            own_piece(3, 0).start()
            own_piece(3, 1).start()
            to_other(1, 3).start()
            to_other(1, 1).start()

        @pl.when(h == 11)
        def _():
            own_piece(2, 0).wait_recv()
            own_piece(2, 1).wait_recv()
            passed_on(2).start()
            to_other(2, 3).start()
            to_other(2, 1).start()
            passed_on(0).wait_recv()
            to_other(0, 2).start()

        @pl.when(h == 14)
        def _():
            own_piece(3, 0).wait_recv()
            own_piece(3, 1).wait_recv()
            passed_on(3).start()
            to_other(3, 3).start()
            to_other(3, 1).start()
            passed_on(1).wait_recv()
            to_other(1, 2).start()

    for copy in locals_in[4:]:
        copy.wait()
    halo_nb.wait_recv()
    halo_cnt.wait_recv()
    NT[...] = N4[...].T

    def first_copy(h):
        return remote(pbuf.at[h, 1 - c], r0.at[h], s0s.at[0], s0r.at[h], (other, x))

    def second_copy(h, d):
        to = lax.rem(pri + d, 4)
        return remote(sb1.at[h, to], r1.at[h, d - 1], s1s.at[d - 1], s1r.at[h], (s + (to - pri) * step1, x))

    def third_copy(h, d):
        to = lax.rem(sec + d, 4)
        return remote(sb2.at[h, to], r2.at[h, d - 1], s2s.at[d - 1], s2r.at[h], (s + (to - sec) * step2, x))

    def last_copy(h, slot):
        if slot < 3:
            half, to, dev = c, lax.rem(x + slot + 1, FSDP), s
        else:
            half, to, dev = 1 - c, lax.rem(x + slot - 3, FSDP), other
        return remote(sb3.at[h, half * 4 + to], r3.at[h, slot], s3s.at[slot], s3r.at[h], (dev, to))

    def landed(ref, sem):
        return pltpu.make_async_copy(ref, ref, sem)

    @pl.loop(0, HEADS + 4)
    def _(t):
        @pl.when(t >= 4)
        def _():
            h = t - 4
            landed(r3.at[h], s3r.at[h]).wait()
            mine = own3[h] + r3[h, 0] + r3[h, 1] + r3[h, 2]
            theirs = r3[h, 3] + r3[h, 4] + r3[h, 5] + r3[h, 6]
            wout[:, pl.ds(pl.multiple_of(c * WIDTH + h * HD, HD), HD)] = mine[0:6]
            wout[:, pl.ds(pl.multiple_of((1 - c) * WIDTH + h * HD, HD), HD)] = theirs[0:6]

        @pl.when((t >= 3) & (t < HEADS + 3))
        def _():
            h = t - 3
            landed(r2.at[h], s2r.at[h]).wait()
            total = sb2[h, sec].astype(F32)
            for d in range(3):
                total += r2[h, d].astype(F32)
            f3[0:48] = total
            for to in range(8):
                sb3[h, to] = f3[pl.ds(6 * to, 8)]
            own3[h] = sb3[h, c * 4 + x]
            for slot in range(7):
                last_copy(h, slot).start()

        @pl.when((t >= 2) & (t < HEADS + 2))
        def _():
            h = t - 2
            landed(r1.at[h], s1r.at[h]).wait()
            total = sb1[h, pri].astype(F32)
            for d in range(3):
                total += r1[h, d].astype(F32)
            sb2[h] = total.astype(BF16)
            for d in range(1, 4):
                third_copy(h, d).start()

        @pl.when((t >= 1) & (t < HEADS + 1))
        def _():
            h = t - 1
            first_copy(h).wait_recv()
            for a in range(4):
                for b in range(4):
                    rows = pl.ds((a * 4 + b) * 48, 48)
                    total = pbuf[h, c, rows].astype(F32) + r0[h, rows].astype(F32)
                    sb1[h, a * (1 - c) + b * c, b * (1 - c) + a * c] = total.astype(BF16)
            for d in range(1, 4):
                second_copy(h, d).start()

        for j in range(PIECES):
            @pl.when(t == j * (HEADS // PIECES))
            def _():
                if j >= 2:
                    passed_on(j).wait_recv()
                    to_other(j, 2).start()
                for d in (1, 2, 3):
                    at = W.at[shard_rows(lax.rem(x + d, FSDP)), piece_cols(1 - c, j)]
                    landed(at, wpr.at[d - 1, j]).wait()

        @pl.when(t < HEADS)
        def _():
            h = t
            cols = head_cols(h)
            wh = jnp.concatenate([W[:, cols], W[:, head_cols(h + HEADS)]], axis=1)
            kvb[...] = dot(N4[...], wh, ((1,), (0,))).astype(BF16)
            for g in range(4):
                rows = pl.ds(GROUP * g, GROUP)
                span = pl.ds(256 * g, 256)
                q = cqb[rows, cols]
                og = ogb[rows, cols]
                kk = kvb[span, 0:HD]
                vv = kvb[span, HD : 2 * HD]
                count = cprev[3:4] if g == 0 else cown[g - 1 : g]
                bias = jnp.where(count >= 2.0, 0.0, NEG)
                bias = jnp.concatenate([jnp.zeros_like(bias), bias], axis=1)
                raw = dot(q, kk, ((1,), (1,))) + bias
                e = jnp.exp2((raw - jnp.max(raw, axis=1, keepdims=True)) * EXP_SCALE)
                inverse = 1.0 / jnp.sum(e, axis=1, keepdims=True)
                if g == 0:
                    inverse = inverse * jnp.where(first, 0.0, 1.0)
                p = e * inverse
                low = p.astype(BF16)
                out = dot(low, vv, ((1,), (0,)))
                bob[rows, cols] = (so[rows, cols] + out).astype(BF16)
                gp = dot(og, vv, ((1,), (1,)))
                sg = (p * (gp - jnp.sum(p * gp, axis=1, keepdims=True))).astype(BF16)
                cgb[rows, cols] = (dot(sg, kk, ((1,), (0,))) * SCALE).astype(BF16)
                kvg[span, 0:HD] = (dot(sg, q, ((0,), (0,))) * SCALE).astype(BF16)
                kvg[span, HD : 2 * HD] = dot(low, og, ((0,), (0,))).astype(BF16)
            part = dot(NT[...], kvg[...], ((1,), (0,)))
            pbuf[h, 0] = part[:, 0:HD].astype(BF16)
            pbuf[h, 1] = part[:, HD : 2 * HD].astype(BF16)
            first_copy(h).start()
            column_out(bob, bo_hbm, 0, h).start()
            column_out(cgb, cg_hbm, 4, h).start()
            grad_return(h).wait_recv()
            kgb[:, cols] = (dko[h] + dpr[h, 0].astype(F32)).astype(BF16)
            vgb[:, cols] = (dvo[h] + dpr[h, 1].astype(F32)).astype(BF16)
            column_out(kgb, kg_hbm, 2, h).start()
            column_out(vgb, vg_hbm, 3, h).start()

    weight_out = pltpu.make_async_copy(wout, wg_hbm, osem.at[5])
    weight_out.start()
    remote(k_hbm, kbuf.at[pl.ds(0, ROWS)], hs.at[0], hr.at[0, 0], (nxt, x)).wait_send()
    remote(v_hbm, vbuf.at[pl.ds(0, ROWS)], hs.at[1], hr.at[1, 0], (nxt, x)).wait_send()
    halo_nb.wait_send()
    halo_cnt.wait_send()
    for j in range(PIECES):
        own_piece(j, 0).wait_send()
        own_piece(j, 1).wait_send()
        passed_on(j).wait_send()
        for d in (1, 2, 3):
            to_other(j, d).wait_send()
    landed(dps, dss.at[0]).wait()
    landed(r0, s0s.at[0]).wait()
    for d in range(3):
        landed(r1.at[:, d], s1s.at[d]).wait()
        landed(r2.at[:, d], s2s.at[d]).wait()
    for slot in range(7):
        landed(r3.at[:, slot], s3s.at[slot]).wait()
    for at, (buf, hbm) in enumerate(((bob, bo_hbm), (qgb, qg_hbm), (kgb, kg_hbm), (vgb, vg_hbm), (cgb, cg_hbm))):
        pltpu.make_async_copy(buf, hbm, osem.at[at]).wait()
    weight_out.wait()


def on_device(
    self_query, self_key, self_value, cross_query, neighbours, neighbour_count, kv_weight, out_grad
):
    counts = jnp.zeros((8, 128), F32) + jnp.pad(neighbour_count[0].astype(F32), (0, 4))[:, None]
    wide = jax.ShapeDtypeStruct((ROWS, WIDTH), BF16)
    token = lambda dtype=BF16: pltpu.VMEM((ROWS, WIDTH), dtype)
    dma = lambda *shape: pltpu.SemaphoreType.DMA(shape)
    anywhere = pl.BlockSpec(memory_space=pl.ANY)
    outs = pl.pallas_call(
        kernel,
        out_shape=[wide] * 5 + [jax.ShapeDtypeStruct((6, 2 * WIDTH), F32)],
        in_specs=[anywhere] * 8,
        out_specs=[anywhere] * 6,
        scratch_shapes=[
            token(), token(), token(),
            pltpu.VMEM((2 * ROWS, WIDTH), BF16), pltpu.VMEM((2 * ROWS, WIDTH), BF16),
            token(F32), token(), token(), token(), token(), token(),
            pltpu.VMEM((HEADS, 2, ROWS, HD), BF16), pltpu.VMEM((HEADS, 2, ROWS, HD), BF16),
            pltpu.VMEM((HEADS, ROWS, HD), F32), pltpu.VMEM((HEADS, ROWS, HD), F32),
            pltpu.VMEM((ENC, 2 * WIDTH), BF16), pltpu.VMEM((1024, ENC), BF16), pltpu.VMEM((ENC, 1024), BF16),
            pltpu.VMEM((8, 128), F32), pltpu.VMEM((8, 128), F32),
            pltpu.VMEM((2, 128, 384), F32),
            pltpu.VMEM((1024, 2 * HD), BF16), pltpu.VMEM((1024, 2 * HD), BF16),
            pltpu.VMEM((HEADS, 2, ENC, HD), BF16), pltpu.VMEM((HEADS, ENC, HD), BF16),
            pltpu.VMEM((HEADS, 4, 4, 48, HD), BF16), pltpu.VMEM((HEADS, 3, 4, 48, HD), BF16),
            pltpu.VMEM((HEADS, 4, 48, HD), BF16), pltpu.VMEM((HEADS, 3, 48, HD), BF16),
            pltpu.VMEM((56, HD), F32), pltpu.VMEM((HEADS, 8, 8, HD), F32),
            pltpu.VMEM((HEADS, 8, HD), F32), pltpu.VMEM((HEADS, 7, 8, HD), F32),
            pltpu.VMEM((6, 2 * WIDTH), F32),
            dma(8), dma(2), dma(2, HEADS), dma(2), dma(2),
            dma(2, PIECES), dma(2, PIECES), dma(PIECES), dma(PIECES), dma(3, PIECES), dma(3, PIECES),
            dma(1), dma(HEADS), dma(6),
            dma(1), dma(HEADS), dma(3), dma(HEADS), dma(3), dma(HEADS), dma(7), dma(HEADS),
        ],
        compiler_params=pltpu.CompilerParams(
            collective_id=0, has_side_effects=True, vmem_limit_bytes=67043328
        ),
    )(
        self_query[0], self_key[0], self_value[0], cross_query[0], neighbours.reshape(1024, ENC),
        counts, kv_weight, out_grad[0],
    )
    return tuple(array[None] for array in outs[:5]) + (outs[5],)


def solution(mesh):
    wide = P("fsdp", "seq", None)
    return jax.shard_map(
        on_device,
        mesh=mesh,
        in_specs=(wide, wide, wide, wide, P("fsdp", "seq", None, None), P("fsdp", "seq"), P("fsdp", None), wide),
        out_specs=(wide, wide, wide, wide, wide, P(("seq", "fsdp"), None)),
        check_vma=False,
    )
```

time: 457 us -> 151 us (0.33)
  matrix products: 142 us -> 0 us
  Pallas kernels: 0 us -> 140 us
  waiting for transfers between devices: 138 us -> 0 us
  local copies, waits for them, and re-layouts: 102 us -> 8.98 us
  other arithmetic: 35.8 us -> 0.66 us
  starting transfers between devices: 20.4 us -> 0 us
  between operations: 14.6 us -> 0.66 us
    dot_general x14 -> x0, matrix products: 142 us -> none  [the longest x2 45.6 us: attend(): jnp.einsum('...hqk,...qhd->...khd', score_grad, queries, preferred_elemen...]
    pallas_call x0 -> x1, Pallas kernels: none -> 140 us  [on_device(): pl.pallas_call(kernel, out_shape=[wide] * 5 + [jax.ShapeDtypeStruct((6, 2...]
    all_gather x1 -> x0, waiting for transfers between devices: 70.4 us -> none  [on_device(): lax.all_gather(kv_weight, 'fsdp', axis=0, tiled=True)]
    unnamed x3 -> x0, waiting for transfers between devices: 56.3 us -> none
    slice x12 -> x0, local copies, waits for them, and re-layouts: 31.1 us -> none  [the longest x2 14.9 us: on_device(): kv_proj = jnp.concatenate([last_proj[None], own_proj[:groups - 1]], 0)]
    unnamed x55 -> x16, local copies, waits for them, and re-layouts: 29.6 us -> 8.31 us
    ppermute x7 -> x0, starting transfers between devices: 20.3 us -> none  [from_behind(): lax.ppermute(value, axis, [(source, source + steps) for source in range(f...]
    reshape x4 -> x0, local copies, waits for them, and re-layouts: 18.2 us -> none  [the longest x1 6.28 us: on_device(): cross_vgrad.reshape(groups, neigh_rows, feature_width)]
  transfers between devices with their start and end apart: 9 -> 0, of which waited for: 3 -> 0; matrix products, arithmetic and copies ran while one was open for 55% -> 0% of each run, Pallas kernels for 0% -> 0%
where the time goes in v1:
time: 151 us; the launch traced here: 150 us
  Pallas kernels  140 us (93%)
  local copies, waits for them, and re-layouts  8.98 us (6%)
    pallas_call x1, Pallas kernels, on_device(): pl.pallas_call(kernel, out_shape=[wide] * 5 + [jax.ShapeDtypeStruct((6, 2...  140 us
    unnamed x16, local copies, waits for them, and re-layouts  8.31 us

profile of v1, /device:TPU:1, one launch (start us, length us, event | category | flops | bytes accessed | tf_op | source)
XLA Modules:
  0.0 150.5 jit_solution(9370883243774009832)
XLA Ops:
  0.6 0.7 convert_bitcast_fusion
  1.3 0.7 add.7.cnt_hbm
  2.0 140.2 %shard_map.127 = (bf16[256,2048]{1,0:T(8,128)(2,1)}, bf16[256,2048]{1,0:T(8,128)(2,1)}, bf16[256,2048]{1,0:T(8,128)(2,1)}, bf16[256,2048]{1,0:T(8,128)(2,1)}, bf...) custom-call(bf16[256,2048]{1,0:T(8,128)(2,1)} %bitcast.19, bf16[256,2048]{1,0:T(8,128)(2,1)} %bitcast.20, ...), custom_call_target="tpu_custom_call" | custom-call | tf_op jit(solution)/shard_map/pallas_call | solution.py:380
  142.2 0.0 copy-start.3
  142.2 0.0 copy-start.2
  142.2 2.5 %copy.20 = bf16[1,256,2048]{2,1,0:T(8,128)(2,1)} copy(bf16[1,256,2048]{2,1,0:T(8,128)(2,1)} %bitcast.18) | data formatting | bytes 2097152
  144.6 0.0 copy-done.3
  144.6 1.0 copy.21
  145.6 0.0 copy-done.2
  145.6 0.0 copy-start.1
  145.6 1.0 copy.22
  146.6 0.6 copy-done.1
  147.2 0.0 copy-start
  147.2 1.0 copy.23
  148.2 0.6 copy-done
  148.8 0.0 copy-start.4
  148.8 1.0 copy.24
  149.8 0.1 copy-done.4
  149.8 0.7 copy.25
  (1 shorter events, 0.0 us)
Async XLA Ops:
  142.2 2.5 %copy-start.3 = (bf16[256,2048]{1,0:T(8,128)(2,1)S(1)}, bf16[256,2048]{1,0:T(8,128)(2,1)}, u32[]{:S(2)}) copy-start(bf16[256,2048]{1,0:T(8,128)(2,1)} %get-tuple-element.13) | copy-start | bytes 3145732
  142.2 3.4 %copy-start.2 = (bf16[256,2048]{1,0:T(8,128)(2,1)S(1)}, bf16[256,2048]{1,0:T(8,128)(2,1)}, u32[]{:S(2)}) copy-start(bf16[256,2048]{1,0:T(8,128)(2,1)} %get-tuple-element.14) | copy-start | bytes 3145732
  145.6 1.6 %copy-start.1 = (bf16[256,2048]{1,0:T(8,128)(2,1)S(1)}, bf16[256,2048]{1,0:T(8,128)(2,1)}, u32[]{:S(2)}) copy-start(bf16[256,2048]{1,0:T(8,128)(2,1)} %get-tuple-element.15) | copy-start | bytes 3145732
  147.2 1.6 %copy-start = (bf16[256,2048]{1,0:T(8,128)(2,1)S(1)}, bf16[256,2048]{1,0:T(8,128)(2,1)}, u32[]{:S(2)}) copy-start(bf16[256,2048]{1,0:T(8,128)(2,1)} %get-tuple-element.16) | copy-start | bytes 3145732
  148.8 1.0 copy-start.4
